TPU v7x, 256 devices: a whole 4x4x8 slice. The times are simulated.
256 devices in a mesh: dp: 8 (over x, core), expert: 32 (over z, y).
Axes of the slice: x: 4, y: 4, z: 8, core: 2. Of those that a mesh axis runs over, the one named last changes fastest.
Arguments:
- tokens: bfloat16 [2048, 3584], P(('dp', 'expert')), may hold values from -6 to 6
- cotangent: bfloat16 [2048, 3584], P(('dp', 'expert')), may hold values from -6 to 6
- routes: int32 [2048, 8], P(('dp', 'expert')), may hold values from 0 to 31, all different within a row; in each aligned block of 8 rows (0 to 7, 8 to 15, ...) at most 3 rows name the same one
- gates: bfloat16 [2048, 8], P(('dp', 'expert')), may hold values from 0.049804688 to 1
- w_gate: bfloat16 [32, 3584, 2048], P('expert', None, 'dp'), may hold values from -0.09375 to 0.09375
- w_up: bfloat16 [32, 3584, 2048], P('expert', None, 'dp'), may hold values from -0.09375 to 0.09375
- w_down: bfloat16 [32, 2048, 3584], P('expert', 'dp'), may hold values from -0.125 to 0.125
Outputs:
- grad_tokens: bfloat16 [2048, 3584], P(('dp', 'expert'))
- grad_gate: bfloat16 [32, 3584, 2048], P('expert', None, 'dp')
- grad_up: bfloat16 [32, 3584, 2048], P('expert', None, 'dp')
- grad_down: bfloat16 [32, 2048, 3584], P('expert', 'dp')
Inputs may be any that keep to these rules, and one draw needn't show every extreme that they name: `routes`: each row names 8 different experts; among the rows of one device no expert is named more than 3 times, a bound that some block reaches.
All inputs are finite; a program needn't handle non-finite values.
Results may differ from a plain program's by a relative error of at most 0.01.
Values may be sent and summed in bfloat16 or wider, within the bound.
No kernel may reach another device: no remote copies, remote signals or barrier semaphores. Data moves between devices by JAX's collectives and lax.ppermute only.
A program may use at most 128 MiB of HBM per device.

v0:
```python
import math
import jax
import jax.numpy as jnp
from jax import lax
from jax.sharding import PartitionSpec as P


def in_one_piece(arrays, axis, split_dim, concat_dim, along):
    widths = [math.prod(a.shape[along:]) for a in arrays]
    both = jnp.concatenate(
        [a.reshape(*a.shape[:along], w) for a, w in zip(arrays, widths)], axis=along
    )
    out = lax.all_to_all(both, axis, split_axis=split_dim, concat_axis=concat_dim, tiled=True)
    parts = jnp.split(out, [sum(widths[:k]) for k in range(1, len(widths))], axis=along)
    return tuple((b.reshape(*out.shape[:along], *a.shape[along:]) for a, b in zip(arrays, parts)))


def slot_index(flat_ids, expert_count):
    onehot = (flat_ids[..., None] == jnp.arange(expert_count, dtype=jnp.int32)).astype(jnp.int32)
    return jnp.sum((jnp.cumsum(onehot, axis=-2) - onehot) * onehot, axis=-1)


def expert_terms(rows_x, rows_dy, gate_rows, gate_mat, up_mat, down_mat):
    gate_pre = jnp.dot(rows_x, gate_mat, preferred_element_type=jnp.float32)
    up_pre = jnp.dot(rows_x, up_mat, preferred_element_type=jnp.float32)
    sigmoid_g = jax.nn.sigmoid(gate_pre)
    activated = gate_pre * sigmoid_g
    gate_scale = gate_rows.astype(jnp.float32)[:, None]
    hidden = (gate_scale * activated * up_pre).astype(jnp.bfloat16)
    returned = gate_scale * jnp.dot(rows_dy, down_mat.T, preferred_element_type=jnp.float32)
    d_gate = (returned * up_pre * sigmoid_g * (1.0 + gate_pre * (1.0 - sigmoid_g))).astype(
        jnp.bfloat16
    )
    d_up = (returned * activated).astype(jnp.bfloat16)
    grad_gate = jnp.dot(rows_x.T, d_gate, preferred_element_type=jnp.float32)
    grad_up = jnp.dot(rows_x.T, d_up, preferred_element_type=jnp.float32)
    grad_down = jnp.dot(hidden.T, rows_dy, preferred_element_type=jnp.float32)
    return (d_gate, d_up, grad_gate, grad_up, grad_down)


def per_device(tokens, cotangent, routes, gates, w_gate, w_up, w_down):
    tok_rows, features = tokens.shape
    top_k = routes.shape[1]
    expert_count = lax.axis_size("expert")
    capacity = min(tok_rows, (3 * tok_rows * top_k + 2 * expert_count - 1) // (2 * expert_count))
    gate_mat = w_gate[0]
    up_mat = w_up[0]
    down_mat = w_down[0]
    flat_ids = routes.reshape(-1)
    position = flat_ids * capacity + slot_index(flat_ids, expert_count)
    token_of = jnp.arange(tok_rows * top_k, dtype=jnp.int32) // top_k
    slots_all = expert_count * capacity
    send_x = jnp.zeros((slots_all, features), jnp.bfloat16).at[position].set(tokens[token_of])
    send_dy = jnp.zeros((slots_all, features), jnp.bfloat16).at[position].set(cotangent[token_of])
    send_gate = jnp.zeros((slots_all,), jnp.bfloat16).at[position].set(gates.reshape(-1))
    received = in_one_piece(
        (
            send_x.reshape(expert_count, capacity, features),
            send_dy.reshape(expert_count, capacity, features),
            send_gate.reshape(expert_count, capacity),
        ),
        "expert",
        0,
        0,
        2,
    )
    gathered = (
        lax.all_gather(received[0], "dp", axis=0, tiled=True),
        lax.all_gather(received[1], "dp", axis=0, tiled=True),
        lax.all_gather(received[2], "dp", axis=0, tiled=True),
    )
    rows_x = gathered[0].reshape(-1, features)
    rows_dy = gathered[1].reshape(-1, features)
    d_gate, d_up, grad_gate, grad_up, grad_down = expert_terms(
        rows_x, rows_dy, gathered[2].reshape(-1), gate_mat, up_mat, down_mat
    )
    own_rows = lax.psum_scatter(
        (
            jnp.dot(d_gate, gate_mat.T, preferred_element_type=jnp.float32)
            + jnp.dot(d_up, up_mat.T, preferred_element_type=jnp.float32)
        ).astype(jnp.bfloat16),
        "dp",
        scatter_dimension=0,
        tiled=True,
    ).astype(jnp.float32)
    returned = lax.all_to_all(
        own_rows.reshape(expert_count, capacity, features).astype(jnp.bfloat16),
        "expert",
        split_axis=0,
        concat_axis=0,
        tiled=True,
    ).astype(jnp.float32)
    selected = returned.reshape(slots_all, features)[position]
    grad_x = selected.reshape(tok_rows, top_k, features).sum(axis=1)
    return (
        grad_x.astype(jnp.bfloat16),
        grad_gate.astype(jnp.bfloat16)[None],
        grad_up.astype(jnp.bfloat16)[None],
        grad_down.astype(jnp.bfloat16)[None],
    )


def solution(mesh):
    return jax.shard_map(
        per_device,
        mesh=mesh,
        in_specs=(
            P(("dp", "expert"), None),
            P(("dp", "expert"), None),
            P(("dp", "expert"), None),
            P(("dp", "expert"), None),
            P("expert", None, "dp"),
            P("expert", None, "dp"),
            P("expert", "dp", None),
        ),
        out_specs=(
            P(("dp", "expert"), None),
            P("expert", None, "dp"),
            P("expert", None, "dp"),
            P("expert", "dp", None),
        ),
        check_vma=False,
    )
```

profile of v0, /device:TPU:15, one launch (start us, length us, event | category | flops | bytes accessed | tf_op | source)
XLA Modules:
  0.0 286.5 jit_solution(9832261786138127804)
XLA Ops:
  7.2 0.0 all-gather.6.cloned.1.call-start
  7.2 0.9 eq.15
  8.1 0.7 broadcast_multiply_fusion
  8.8 0.1 fusion.24
  8.9 0.1 reduce_window_sum.11
  9.0 0.2 select_reduce_fusion
  9.2 0.1 mul.58
  9.3 4.0 %scatter_custom_fusion = bf16[96,3584]{1,0:T(8,128)(2,1)S(1)} fusion(s32[64]{0:T(128)S(1)} %fusion.26, bf16[8,3584]{1,0:T(8,128)(2,1)} %param.7, s32[1024]{0:T(1024)S(1)} %pad_clamp_fusion.1, bf16[]{:T(256)} %constant.26.clone.1), kind=kCustom, calls=%fused_computation.32 | custom fusion | bytes 688640 | tf_op jit(solution)/shard_map/scatter | solution.py:53
  13.3 0.4 reshape.118
  13.7 4.0 %scatter_custom_fusion.1 = bf16[96,3584]{1,0:T(8,128)(2,1)S(1)} fusion(s32[64]{0:T(128)S(1)} %fusion.26, bf16[8,3584]{1,0:T(8,128)(2,1)} %param.8, s32[1024]{0:T(1024)S(1)} %pad_clamp_fusion.1, bf16[]{:T(256)} %constant.26.clone.1), kind=kCustom, calls=%fused_computation.30 | custom fusion | bytes 688640 | tf_op jit(solution)/shard_map/scatter | solution.py:54
  17.7 1.2 reshape.119
  18.8 0.1 reshape.174
  18.9 1.0 scatter_custom_fusion.2
  19.9 0.2 reshape_reshape.4
  20.1 1.9 pad_maximum_fusion
  22.0 55.3 %all_to_all.10 = bf16[32,3,7169]{2,1,0:T(4,128)(2,1)S(1)} all-to-all(bf16[32,3,7169]{2,1,0:T(4,128)(2,1)S(1)} %pad_maximum_fusion), channel_id=1, replica_groups=mesh['dp'=8,'expert'=32] {'expert'}, dimensions={0} | all-to-all | bytes 2752896 | tf_op jit(solution)/shard_map/all_to_all | solution.py:13
  77.3 1.3 copy-done.1
  78.6 0.6 fusion.30
  79.3 1.0 copy.17
  80.3 0.0 all-gather.4.cloned.1.call-start
  80.3 1.0 copy.15
  81.4 0.0 reduce-scatter.2.cloned.1.call-start
  81.4 0.3 copy.14
  81.7 15.5 %all-gather = bf16[256,3,1]{1,2,0:T(2,128)(2,1)S(1)} all-gather(bf16[32,3,1]{1,2,0:T(2,128)(2,1)S(1)} %copy.14), channel_id=2, replica_groups=mesh['dp'=8,'expert'=32] {'dp'}, dimensions={0}, use_global_device_ids=true | all-gather | bytes 1728 | tf_op jit(solution)/shard_map/all_gather | solution.py:70
  97.2 0.4 convert_reduce_fusion
  97.6 0.2 reshape.127
  97.8 19.9 %all-gather.6.cloned.1.call-done = bf16[256,3,3584]{2,0,1:T(8,128)(2,1)} async-done(((bf16[32,3,3584]{2,0,1:T(8,128)(2,1)}), bf16[256,3,3584]{2,0,1:T(8,128)(2,1)}) %all-gather.6.cloned.1.call-update) | async-done | bytes 5505040 | tf_op jit(solution)/shard_map/all_gather | solution.py:68
  117.7 10.2 %copy.18 = bf16[256,3,3584]{2,1,0:T(4,128)(2,1)} copy(bf16[256,3,3584]{2,0,1:T(8,128)(2,1)} %all-gather.6.cloned.1.call-done) | data formatting | bytes 11010048 | tf_op jit(solution)/shard_map/all_gather | solution.py:68
  127.9 13.1 %reshape.123 = bf16[768,3584]{1,0:T(8,128)(2,1)} reshape(bf16[256,3,3584]{2,1,0:T(4,128)(2,1)} %copy.18) | data formatting | bytes 11010048 | tf_op jit(solution)/shard_map/reshape | solution.py:72
  141.0 4.4 %fusion.5 = f32[768,256]{1,0:T(8,128)S(1)} fusion(bf16[768,3584]{1,0:T(8,128)(2,1)} %reshape.123, bf16[1,3584,256]{2,1,0:T(8,128)(2,1)S(1)} %copy-done), kind=kOutput, calls=%fused_computation.16 | convolution fusion | flops 1409286144 | bytes 8126464 | tf_op jit(solution)/shard_map/dot_general | solution.py:24
  145.4 0.6 copy-done.3
  146.0 2.5 fusion.8
  148.4 11.7 %all-gather.4.cloned.1.call-done = bf16[256,3,3584]{2,0,1:T(8,128)(2,1)} async-done(((bf16[32,3,3584]{2,0,1:T(8,128)(2,1)}), bf16[256,3,3584]{2,0,1:T(8,128)(2,1)}) %all-gather.4.cloned.1.call-update) | async-done | bytes 5505040 | tf_op jit(solution)/shard_map/all_gather | solution.py:69
  160.1 10.2 %copy.16 = bf16[256,3,3584]{2,1,0:T(4,128)(2,1)} copy(bf16[256,3,3584]{2,0,1:T(8,128)(2,1)} %all-gather.4.cloned.1.call-done) | data formatting | bytes 11010048 | tf_op jit(solution)/shard_map/all_gather | solution.py:69
  170.4 13.0 %reshape.122 = bf16[768,3584]{1,0:T(8,128)(2,1)} reshape(bf16[256,3,3584]{2,1,0:T(4,128)(2,1)} %copy.16) | data formatting | bytes 11010048 | tf_op jit(solution)/shard_map/reshape | solution.py:73
  183.4 5.0 %multiply_convert_fusion.1 = (bf16[768,256]{1,0:T(8,128)(2,1)S(1)}, bf16[768,256]{1,0:T(8,128)(2,1)S(1)}) fusion(f32[768,256]{1,0:T(8,128)S(1)} %fusion.5, f32[768,256]{1,0:T(8,128)} %fusion.8, bf16[768,3584]{1,0:T(8,128)(2,1)} %reshape.122, bf16[1,256,3584]{2,1,0:T(8,128)(2,1)} %param.13, f32[768]{0:T(1024)S(1)} %reshape.127), kind=kOutput, calls=%fused_computation.26 | convolution fusion | flops 1412038656 | bytes 9702400 | tf_op jit(solution)/shard_map/dot_general | solution.py:30
  188.4 1.6 fusion.3
  190.1 4.0 %add_convert_fusion = bf16[768,3584]{1,0:T(8,128)(2,1)} fusion(f32[768,3584]{1,0:T(8,128)S(1)} %fusion.3, bf16[768,256]{1,0:T(8,128)(2,1)S(1)} %get-tuple-element.6, bf16[1,3584,256]{2,1,0:T(8,128)(2,1)S(1)} %copy-done.4), kind=kOutput, calls=%fused_computation.6 | convolution fusion | flops 1414791168 | bytes 18743296 | tf_op jit(solution)/shard_map/dot_general | solution.py:80
  194.2 43.8 %reduce-scatter.2.cloned.1.call-done = bf16[96,3584]{1,0:T(8,128)(2,1)} async-done(((bf16[768,3584]{1,0:T(8,128)(2,1)}), bf16[96,3584]{1,0:T(8,128)(2,1)}) %reduce-scatter.2.cloned.1.call-update) | async-done | bytes 688144 | tf_op jit(solution)/shard_map/reduce_scatter | solution.py:77
  238.0 2.1 convert_element_type.49
  240.1 9.7 %all-to-all-start.1 = ((bf16[32,3,3584]{2,1,0:T(4,128)(2,1)}), bf16[32,3,3584]{2,1,0:T(4,128)(2,1)}, u32[]{:S(2)}, u32[]{:S(2)}) async-start(bf16[32,3,3584]{2,1,0:T(4,128)(2,1)} %convert_element_type.49), calls=%async_computation.2 | async-start | bytes 1835008 | tf_op jit(solution)/shard_map/all_to_all | solution.py:86
  249.9 5.6 %fusion.1 = bf16[1,3584,256]{2,1,0:T(8,128)(2,1)} fusion(bf16[768,3584]{1,0:T(8,128)(2,1)} %reshape.123, bf16[768,256]{1,0:T(8,128)(2,1)} %copy-done.5), kind=kOutput, calls=%fused_computation.11 | convolution fusion | flops 1410203648 | bytes 7733248 | tf_op jit(solution)/shard_map/dot_general | solution.py:36
  255.5 2.9 %fusion = bf16[1,3584,256]{2,1,0:T(8,128)(2,1)} fusion(bf16[768,3584]{1,0:T(8,128)(2,1)S(1)} %bitcast.44, bf16[768,256]{1,0:T(8,128)(2,1)S(1)} %get-tuple-element.7), kind=kOutput, calls=%fused_computation.10 | convolution fusion | flops 1410203648 | bytes 7733248 | tf_op jit(solution)/shard_map/dot_general | solution.py:35
  258.4 3.0 %fusion.2 = bf16[1,256,3584]{2,1,0:T(8,128)(2,1)} fusion(bf16[768,3584]{1,0:T(8,128)(2,1)S(1)} %bitcast.46, f32[768,256]{1,0:T(8,128)S(1)} %copy-done.9, f32[768]{0:T(1024)S(1)} %reshape.127, f32[768,256]{1,0:T(8,128)S(1)} %copy-done.8), kind=kOutput, calls=%fused_computation.12 | convolution fusion | flops 1411579904 | bytes 8915968 | tf_op jit(solution)/shard_map/dot_general | solution.py:37
  261.5 13.1 %all-to-all-done.1 = bf16[32,3,3584]{2,1,0:T(4,128)(2,1)} async-done(((bf16[32,3,3584]{2,1,0:T(4,128)(2,1)}), bf16[32,3,3584]{2,1,0:T(4,128)(2,1)}, u32[]{:S(2)}, u32[]{:S(2)}) %all-to-all-start.1) | async-done | bytes 688160 | tf_op jit(solution)/shard_map/all_to_all | solution.py:86
  274.6 1.6 reshape.129
  276.1 1.8 gather_fusion
  277.9 2.0 bitcast_reduce_fusion
  (37 shorter events, 0.1 us)
Async XLA Ops:
  7.2 133.8 %copy-start = (bf16[1,3584,256]{2,1,0:T(8,128)(2,1)S(1)}, bf16[1,3584,256]{2,1,0:T(8,128)(2,1)}, u32[]{:S(2)}) copy-start(bf16[1,3584,256]{2,1,0:T(8,128)(2,1)} %param.11) | copy-start | bytes 5505028
  7.2 11.7 %copy-start.6 = (bf16[8,8]{1,0:T(8,128)(2,1)S(1)}, bf16[8,8]{1,0:T(8,128)(2,1)}, u32[]{:S(2)}) copy-start(bf16[8,8]{1,0:T(8,128)(2,1)} %param.10) | copy-start | bytes 388
  7.2 110.5 %all-gather.6.cloned.1.call-start = ((), (), s32[]{:S(2)}) async-start(), calls=%async_computation.4 | async-start | bytes 6193152 | tf_op jit(solution)/shard_map/all_gather | solution.py:68
  77.3 1.3 copy-start.1
  79.3 2.2 slice-start
  80.3 79.9 %all-gather.4.cloned.1.call-start = ((), (), s32[]{:S(2)}) async-start(), calls=%async_computation.3 | async-start | bytes 6193152 | tf_op jit(solution)/shard_map/all_gather | solution.py:69
  81.4 156.6 %reduce-scatter.2.cloned.1.call-start = ((), (), s32[]{:S(2)}) async-start(), calls=%async_computation.5 | async-start | bytes 6193152 | tf_op jit(solution)/shard_map/reduce_scatter | solution.py:77
  141.0 4.4 %copy-start.2 = (bf16[768,3584]{1,0:T(8,128)(2,1)S(1)}, bf16[768,3584]{1,0:T(8,128)(2,1)}, u32[]{:S(2)}) copy-start(bf16[768,3584]{1,0:T(8,128)(2,1)} %reshape.123) | copy-start | bytes 16515076
  141.0 5.0 %copy-start.3 = (bf16[1,3584,256]{2,1,0:T(8,128)(2,1)S(1)}, bf16[1,3584,256]{2,1,0:T(8,128)(2,1)}, u32[]{:S(2)}) copy-start(bf16[1,3584,256]{2,1,0:T(8,128)(2,1)} %param.12) | copy-start | bytes 5505028
  146.0 37.4 %copy-start.7 = (f32[768,256]{1,0:T(8,128)}, f32[768,256]{1,0:T(8,128)S(1)}, u32[]{:S(2)}) copy-start(f32[768,256]{1,0:T(8,128)S(1)} %fusion.5) | copy-start | bytes 2359300
  188.4 1.7 copy-start.5
  188.4 1.7 copy-start.4
  240.1 15.4 %slice-start.1 = ((s8[5505024]{0:T(1024)(128)(4,1)}), s8[1310720]{0:T(1024)(128)(4,1)S(1)}, s32[]{:S(2)}) async-start(s8[5505024]{0:T(1024)(128)(4,1)} %bitcast.43), calls=%async_computation.7 | async-start | bytes 2621440
  240.1 34.5 %all-to-all-start.1 = ((bf16[32,3,3584]{2,1,0:T(4,128)(2,1)}), bf16[32,3,3584]{2,1,0:T(4,128)(2,1)}, u32[]{:S(2)}, u32[]{:S(2)}) async-start(bf16[32,3,3584]{2,1,0:T(4,128)(2,1)} %convert_element_type.49), calls=%async_computation.2 | async-start | bytes 1835008 | tf_op jit(solution)/shard_map/all_to_all | solution.py:86
  249.8 5.7 %slice-start.2 = ((s8[5505024]{0:T(1024)(128)(4,1)}), s8[4194304]{0:T(1024)(128)(4,1)S(1)}, s32[]{:S(2)}) async-start(s8[5505024]{0:T(1024)(128)(4,1)} %bitcast.43), calls=%async_computation.8 | async-start | bytes 8388608
  249.8 8.6 %slice-start.3 = ((s8[5505024]{0:T(1024)(128)(4,1)}), s8[4194304]{0:T(1024)(128)(4,1)S(1)}, s32[]{:S(2)}) async-start(s8[5505024]{0:T(1024)(128)(4,1)} %bitcast.45), calls=%async_computation.9 | async-start | bytes 8388608
  255.5 2.9 %slice-start.4 = ((s8[5505024]{0:T(1024)(128)(4,1)}), s8[1310720]{0:T(1024)(128)(4,1)S(1)}, s32[]{:S(2)}) async-start(s8[5505024]{0:T(1024)(128)(4,1)} %bitcast.45), calls=%async_computation.10 | async-start | bytes 2621440
  255.5 2.9 %copy-start.8 = (f32[768,256]{1,0:T(8,128)S(1)}, f32[768,256]{1,0:T(8,128)}, u32[]{:S(2)}) copy-start(f32[768,256]{1,0:T(8,128)} %copy-done.7) | copy-start | bytes 2359300
  255.5 2.9 %copy-start.9 = (f32[768,256]{1,0:T(8,128)S(1)}, f32[768,256]{1,0:T(8,128)}, u32[]{:S(2)}) copy-start(f32[768,256]{1,0:T(8,128)} %fusion.8) | copy-start | bytes 2359300
Sparse Core Ops, SparseCore 0:
  80.4 37.1 all-gather.5
  120.1 40.0 all-gather.3
  194.3 43.6 reduce-scatter.1
where the time goes:
time: 288 us; the launch traced here: 286 us
  waiting for transfers between devices  88.5 us (31%)
  blocking collectives  70.8 us (25%)
  local copies, waits for them, and re-layouts  68.8 us (24%)
  matrix products  29.1 us (10%)
  between operations  14 us (5%)
  starting transfers between devices  9.84 us (3%)
  other arithmetic  5.39 us (2%)
    all_to_all x1, blocking collectives, in_one_piece(): lax.all_to_all(both, axis, split_axis=split_dim, concat_axis=concat_dim,...  55.3 us
    reduce_scatter x1, waiting for transfers between devices, per_device(): lax.psum_scatter((jnp.dot(d_gate, gate_mat.T, preferred_element_type=jnp....  43.8 us
    all_gather x1, waiting for transfers between devices, per_device(): lax.all_gather(received[0], 'dp', axis=0, tiled=True)  19.9 us
    all_gather x1, blocking collectives, per_device(): lax.all_gather(received[2], 'dp', axis=0, tiled=True)  15.5 us
    reshape x1, local copies, waits for them, and re-layouts, per_device(): rows_x = gathered[0].reshape(-1, features)  13.1 us
    all_to_all x1, waiting for transfers between devices, per_device(): lax.all_to_all(own_rows.reshape(expert_count, capacity, features).astype(...  13.1 us
    reshape x1, local copies, waits for them, and re-layouts, per_device(): rows_dy = gathered[1].reshape(-1, features)  13 us
    all_gather x1, waiting for transfers between devices, per_device(): lax.all_gather(received[1], 'dp', axis=0, tiled=True)  11.7 us
  transfers between devices with their start and end apart: 4, of which 4 were waited for; matrix products, arithmetic and copies ran while one was open for 15% of the time, Pallas kernels for 0%

commit v1 on v0

--- a/solution.py
+++ b/solution.py
@@ -3,6 +3,28 @@
 import jax.numpy as jnp
 from jax import lax
 from jax.sharding import PartitionSpec as P
+
+
+def joined_along(pieces, dim):
+    dims = list(pieces.shape[1:])
+    dims[dim] *= pieces.shape[0]
+    return jnp.moveaxis(pieces, 0, dim).reshape(dims)
+
+
+def collect(value, axis, dim):
+    size = lax.axis_size(axis)
+    pairs = [(i, (i + 1) % size) for i in range(size)]
+    back = [(b, a) for a, b in pairs]
+    lower, upper = ([], [])
+    for step in range(size - 1):
+        if step % 2 == 0:
+            lower.append(lax.ppermute(lower[-1] if lower else value, axis, pairs))
+        else:
+            upper.append(lax.ppermute(upper[-1] if upper else value, axis, back))
+    blocks = jnp.stack([*lower[::-1], value, *upper])
+    shift = lax.axis_index(axis) - len(lower)
+    blocks = blocks[(jnp.arange(size) - shift) % size]
+    return joined_along(blocks, dim)
 
 
 def in_one_piece(arrays, axis, split_dim, concat_dim, along):
@@ -66,7 +88,7 @@
     )
     gathered = (
         lax.all_gather(received[0], "dp", axis=0, tiled=True),
-        lax.all_gather(received[1], "dp", axis=0, tiled=True),
+        collect(received[1], "dp", 0),
         lax.all_gather(received[2], "dp", axis=0, tiled=True),
     )
     rows_x = gathered[0].reshape(-1, features)

time: 288 us -> 322 us (1.12)
  local copies, waits for them, and re-layouts: 68.8 us -> 88 us
  starting transfers between devices: 9.84 us -> 23.6 us
    ppermute x0 -> x7, waiting for transfers between devices: none -> 37.3 us  [the longest x4 33.2 us: collect(): lower.append(lax.ppermute(lower[-1] if lower else value, axis, pairs))]
    all_gather x1, waiting for transfers between devices: 19.9 us -> 0.01 us  [per_device(): lax.all_gather(received[0], 'dp', axis=0, tiled=True)]
    unnamed x28 -> x41, local copies, waits for them, and re-layouts: 1.9 us -> 17.4 us
    another operation x0 -> x2, local copies, waits for them, and re-layouts: none -> 14.5 us  [the longest x1 13 us: per_device(): rows_dy = gathered[1].reshape(-1, features)]
    ppermute x0 -> x7, starting transfers between devices: none -> 13.9 us  [the longest x4 13.7 us: collect(): lower.append(lax.ppermute(lower[-1] if lower else value, axis, pairs))]
    reshape x1 -> x0, local copies, waits for them, and re-layouts: 13 us -> none  [per_device(): rows_dy = gathered[1].reshape(-1, features)]
    all_gather x1 -> x0, waiting for transfers between devices: 11.7 us -> none  [per_device(): lax.all_gather(received[1], 'dp', axis=0, tiled=True)]
    gather x0 -> x1, local copies, waits for them, and re-layouts: none -> 11.7 us  [collect(): blocks = blocks[(jnp.arange(size) - shift) % size]]
  transfers between devices with their start and end apart: 4 -> 10, of which waited for: 4 -> 6; matrix products, arithmetic and copies ran while one was open for 15% -> 18% of each run, Pallas kernels for 0% -> 0%
where the time goes in v1:
time: 322 us; the launch traced here: 320 us
  waiting for transfers between devices  90.9 us (28%)
  local copies, waits for them, and re-layouts  88 us (27%)
  blocking collectives  71 us (22%)
  matrix products  26.7 us (8%)
  starting transfers between devices  23.6 us (7%)
  between operations  14.4 us (4%)
  other arithmetic  5.42 us (2%)
    all_to_all x1, blocking collectives, in_one_piece(): lax.all_to_all(both, axis, split_axis=split_dim, concat_axis=concat_dim,...  55.3 us
    reduce_scatter x1, waiting for transfers between devices, per_device(): lax.psum_scatter((jnp.dot(d_gate, gate_mat.T, preferred_element_type=jnp....  40.4 us
    ppermute x4, waiting for transfers between devices, collect(): lower.append(lax.ppermute(lower[-1] if lower else value, axis, pairs))  33.2 us
    unnamed x41, local copies, waits for them, and re-layouts  17.4 us
    all_gather x1, blocking collectives, per_device(): lax.all_gather(received[2], 'dp', axis=0, tiled=True)  15.7 us
    ppermute x4, starting transfers between devices, collect(): lower.append(lax.ppermute(lower[-1] if lower else value, axis, pairs))  13.7 us
    all_to_all x1, waiting for transfers between devices, per_device(): lax.all_to_all(own_rows.reshape(expert_count, capacity, features).astype(...  13.1 us
    reshape x1, local copies, waits for them, and re-layouts, per_device(): rows_x = gathered[0].reshape(-1, features)  13 us
  transfers between devices with their start and end apart: 10, of which 6 were waited for; matrix products, arithmetic and copies ran while one was open for 18% of the time, Pallas kernels for 0%

profile of v1, /device:TPU:15, one launch (start us, length us, event | category | flops | bytes accessed | tf_op | source)
XLA Modules:
  0.0 320.1 jit_solution(16097185435392169966)
XLA Ops:
  7.2 0.9 eq.17
  8.1 0.7 broadcast_multiply_fusion
  9.3 4.0 %scatter_custom_fusion = bf16[96,3584]{1,0:T(8,128)(2,1)S(1)} fusion(s32[64]{0:T(128)S(1)} %fusion.27, bf16[8,3584]{1,0:T(8,128)(2,1)} %param.7, s32[1024]{0:T(1024)S(1)} %pad_clamp_fusion.2, bf16[]{:T(256)} %constant.45.clone.1), kind=kCustom, calls=%fused_computation.41 | custom fusion | bytes 688640 | tf_op jit(solution)/shard_map/scatter | solution.py:75
  13.7 4.0 %scatter_custom_fusion.1 = bf16[96,3584]{1,0:T(8,128)(2,1)S(1)} fusion(s32[64]{0:T(128)S(1)} %fusion.27, bf16[8,3584]{1,0:T(8,128)(2,1)} %param.8, s32[1024]{0:T(1024)S(1)} %pad_clamp_fusion.2, bf16[]{:T(256)} %constant.45.clone.1), kind=kCustom, calls=%fused_computation.39 | custom fusion | bytes 688640 | tf_op jit(solution)/shard_map/scatter | solution.py:76
  17.7 1.2 reshape.165
  18.8 0.8 reshape.227
  19.6 1.0 scatter_custom_fusion.2
  20.8 1.9 pad_maximum_fusion
  22.7 55.3 %all_to_all.10 = bf16[32,3,7169]{2,1,0:T(4,128)(2,1)S(1)} all-to-all(bf16[32,3,7169]{2,1,0:T(4,128)(2,1)S(1)} %pad_maximum_fusion), channel_id=1, replica_groups=mesh['dp'=8,'expert'=32] {'expert'}, dimensions={0} | all-to-all | bytes 2752896 | tf_op jit(solution)/shard_map/all_to_all | solution.py:35
  78.0 1.3 copy-done.1
  80.1 2.6 collective-permute-start
  82.6 7.9 %collective-permute-done = bf16[32,3,3584]{2,0,1:T(8,128)(2,1)S(1)} collective-permute-done((bf16[32,3,3584]{2,0,1:T(8,128)(2,1)S(1)}, bf16[32,3,3584]{2,0,1:T(8,128)(2,1)S(1)}, u32[]{:S(2)}, u32[]{:S(2)}) %collective-permute-start) | collective-permute-done | bytes 688160 | tf_op jit(solution)/shard_map/ppermute | solution.py:21
  90.5 3.7 %collective-permute-start.1 = (bf16[32,3,3584]{2,0,1:T(8,128)(2,1)S(1)}, bf16[32,3,3584]{2,0,1:T(8,128)(2,1)S(1)}, u32[]{:S(2)}, u32[]{:S(2)}) collective-permute-start(bf16[32,3,3584]{2,0,1:T(8,128)(2,1)S(1)} %collective-permute-done), channel_id=1, source_target_pairs={{0,32},{32,64},{64,96},{96,128},{128,160},{160,192},{192,224},{224... | collective-permute-start | bytes 2064392 | tf_op jit(solution)/shard_map/ppermute | solution.py:21
  94.2 1.0 copy.24
  95.3 6.8 %collective-permute-done.1 = bf16[32,3,3584]{2,0,1:T(8,128)(2,1)S(1)} collective-permute-done((bf16[32,3,3584]{2,0,1:T(8,128)(2,1)S(1)}, bf16[32,3,3584]{2,0,1:T(8,128)(2,1)S(1)}, u32[]{:S(2)}, u32[]{:S(2)}) %collective-permute-start.1) | collective-permute-done | bytes 688160 | tf_op jit(solution)/shard_map/ppermute | solution.py:21
  102.1 3.7 %collective-permute-start.2 = (bf16[32,3,3584]{2,0,1:T(8,128)(2,1)S(1)}, bf16[32,3,3584]{2,0,1:T(8,128)(2,1)}, u32[]{:S(2)}, u32[]{:S(2)}) collective-permute-start(bf16[32,3,3584]{2,0,1:T(8,128)(2,1)S(1)} %collective-permute-done.1), channel_id=1, source_target_pairs={{0,32},{32,64},{64,96},{96,128},{128,160},{160,192},{192,224},{224... | collective-permute-start | bytes 2064392 | tf_op jit(solution)/shard_map/ppermute | solution.py:21
  105.8 4.1 %collective-permute-done.4 = bf16[32,3,3584]{2,0,1:T(8,128)(2,1)} collective-permute-done((bf16[32,3,3584]{2,0,1:T(8,128)(2,1)}, bf16[32,3,3584]{2,0,1:T(8,128)(2,1)}, u32[]{:S(2)}, u32[]{:S(2)}) %collective-permute-start.4) | collective-permute-done | bytes 688160 | tf_op jit(solution)/shard_map/ppermute | solution.py:23
  109.9 18.5 %collective-permute-done.2 = bf16[32,3,3584]{2,0,1:T(8,128)(2,1)} collective-permute-done((bf16[32,3,3584]{2,0,1:T(8,128)(2,1)S(1)}, bf16[32,3,3584]{2,0,1:T(8,128)(2,1)}, u32[]{:S(2)}, u32[]{:S(2)}) %collective-permute-start.2) | collective-permute-done | bytes 688160 | tf_op jit(solution)/shard_map/ppermute | solution.py:21
  128.5 3.8 %collective-permute-start.3 = (bf16[32,3,3584]{2,0,1:T(8,128)(2,1)}, bf16[32,3,3584]{2,0,1:T(8,128)(2,1)}, u32[]{:S(2)}, u32[]{:S(2)}) collective-permute-start(bf16[32,3,3584]{2,0,1:T(8,128)(2,1)} %collective-permute-done.2), channel_id=1, source_target_pairs={{0,32},{32,64},{64,96},{96,128},{128,160},{160,192},{192,224},{224... | collective-permute-start | bytes 2064392 | tf_op jit(solution)/shard_map/ppermute | solution.py:21
  132.3 0.8 split.12
  133.4 15.7 %all-gather = bf16[256,3,1]{1,2,0:T(2,128)(2,1)S(1)} all-gather(bf16[32,3,1]{1,2,0:T(2,128)(2,1)S(1)} %copy.14), channel_id=2, replica_groups=mesh['dp'=8,'expert'=32] {'dp'}, dimensions={0}, use_global_device_ids=true | all-gather | bytes 1728 | tf_op jit(solution)/shard_map/all_gather | solution.py:92
  149.8 2.6 bitcast_dynamic-update-slice_fusion.7
  152.5 2.6 bitcast_dynamic-update-slice_fusion.6
  155.1 1.6 bitcast_dynamic-update-slice_fusion.5
  156.6 1.6 bitcast_dynamic-update-slice_fusion.4
  158.2 2.4 bitcast_dynamic-update-slice_fusion.3
  160.7 2.6 bitcast_dynamic-update-slice_fusion.2
  163.3 2.6 bitcast_dynamic-update-slice_fusion.1
  165.9 1.6 bitcast_dynamic-update-slice_fusion
  167.5 11.7 %gather_fusion = bf16[8,32,3,3584]{3,2,1,0:T(4,128)(2,1)} fusion(bf16[8,32,3,3584]{3,2,1,0:T(4,128)(2,1)} %bitcast_dynamic-update-slice_fusion, s32[1024]{0:T(1024)S(1)} %pad_clamp_fusion.1), kind=kCustom, calls=%fused_computation.2 | custom fusion | bytes 11010080 | tf_op jit(solution)/shard_map/gather | solution.py:26
  179.1 13.0 %reshape_reshape.7 = bf16[768,3584]{1,0:T(8,128)(2,1)} reshape(bf16[8,32,3,3584]{3,2,1,0:T(4,128)(2,1)} %gather_fusion) | data formatting | bytes 11010048 | tf_op jit(solution)/shard_map/reshape;reshape | solution.py:95
  192.1 10.3 %copy.25 = bf16[256,3,3584]{2,1,0:T(4,128)(2,1)} copy(bf16[256,3,3584]{2,0,1:T(8,128)(2,1)} %all-gather.3.cloned.1.call-done) | data formatting | bytes 11010048 | tf_op jit(solution)/shard_map/all_gather | solution.py:90
  202.4 13.0 %reshape.168 = bf16[768,3584]{1,0:T(8,128)(2,1)} reshape(bf16[256,3,3584]{2,1,0:T(4,128)(2,1)} %copy.25) | data formatting | bytes 11010048 | tf_op jit(solution)/shard_map/reshape | solution.py:94
  215.4 4.3 %fusion.5 = f32[768,256]{1,0:T(8,128)S(1)} fusion(bf16[768,3584]{1,0:T(8,128)(2,1)} %reshape.168, bf16[1,3584,256]{2,1,0:T(8,128)(2,1)S(1)} %copy-done), kind=kOutput, calls=%fused_computation.17 | convolution fusion | flops 1409286144 | bytes 8126464 | tf_op jit(solution)/shard_map/dot_general | solution.py:46
  219.8 3.5 %fusion.8 = f32[768,256]{1,0:T(8,128)S(1)} fusion(bf16[768,3584]{1,0:T(8,128)(2,1)S(1)} %copy-done.2, bf16[1,3584,256]{2,1,0:T(8,128)(2,1)} %param.12), kind=kOutput, calls=%fused_computation.20 | convolution fusion | flops 1409286144 | bytes 8126464 | tf_op jit(solution)/shard_map/dot_general | solution.py:47
  223.3 1.8 multiply_convert_fusion.1
  225.2 1.6 fusion.3
  226.8 4.0 %add_convert_fusion = bf16[768,3584]{1,0:T(8,128)(2,1)} fusion(f32[768,3584]{1,0:T(8,128)S(1)} %fusion.3, bf16[768,256]{1,0:T(8,128)(2,1)S(1)} %get-tuple-element.6, bf16[1,3584,256]{2,1,0:T(8,128)(2,1)S(1)} %copy-done.3), kind=kOutput, calls=%fused_computation.7 | convolution fusion | flops 1414791168 | bytes 18743296 | tf_op jit(solution)/shard_map/dot_general | solution.py:102
  230.8 40.4 %reduce-scatter.2.cloned.1.call-done = bf16[96,3584]{1,0:T(8,128)(2,1)} async-done(((bf16[768,3584]{1,0:T(8,128)(2,1)}), bf16[96,3584]{1,0:T(8,128)(2,1)}) %reduce-scatter.2.cloned.1.call-update) | async-done | bytes 688144 | tf_op jit(solution)/shard_map/reduce_scatter | solution.py:99
  271.3 2.3 convert_element_type.49
  273.5 9.6 %all-to-all-start.1 = ((bf16[32,3,3584]{2,1,0:T(4,128)(2,1)}), bf16[32,3,3584]{2,1,0:T(4,128)(2,1)}, u32[]{:S(2)}, u32[]{:S(2)}) async-start(bf16[32,3,3584]{2,1,0:T(4,128)(2,1)} %convert_element_type.49), calls=%async_computation.2 | async-start | bytes 1835008 | tf_op jit(solution)/shard_map/all_to_all | solution.py:108
  283.2 5.6 %fusion.1 = bf16[1,3584,256]{2,1,0:T(8,128)(2,1)} fusion(bf16[768,3584]{1,0:T(8,128)(2,1)} %reshape.168, bf16[768,256]{1,0:T(8,128)(2,1)} %copy-done.5), kind=kOutput, calls=%fused_computation.12 | convolution fusion | flops 1410203648 | bytes 7733248 | tf_op jit(solution)/shard_map/dot_general | solution.py:58
  288.9 2.9 fusion
  291.8 3.0 fusion.2
  294.8 13.1 %all-to-all-done.1 = bf16[32,3,3584]{2,1,0:T(4,128)(2,1)} async-done(((bf16[32,3,3584]{2,1,0:T(4,128)(2,1)}), bf16[32,3,3584]{2,1,0:T(4,128)(2,1)}, u32[]{:S(2)}, u32[]{:S(2)}) %all-to-all-start.1) | async-done | bytes 688160 | tf_op jit(solution)/shard_map/all_to_all | solution.py:108
  307.9 1.6 reshape.174
  309.5 1.8 gather_fusion.1
  311.2 2.0 bitcast_reduce_fusion
  (64 shorter events, 3.1 us)
Async XLA Ops:
  7.2 208.3 %copy-start = (bf16[1,3584,256]{2,1,0:T(8,128)(2,1)S(1)}, bf16[1,3584,256]{2,1,0:T(8,128)(2,1)}, u32[]{:S(2)}) copy-start(bf16[1,3584,256]{2,1,0:T(8,128)(2,1)} %param.11) | copy-start | bytes 5505028
  7.2 184.9 %all-gather.3.cloned.1.call-start = ((), (), s32[]{:S(2)}) async-start(), calls=%async_computation.3 | async-start | bytes 6193152 | tf_op jit(solution)/shard_map/all_gather | solution.py:90
  78.0 1.3 copy-start.1
  80.1 10.5 %copy-start.4 = (bf16[32,3,3584]{2,0,1:T(8,128)(2,1)}, bf16[32,3,3584]{2,0,1:T(8,128)(2,1)S(1)}, u32[]{:S(2)}) copy-start(bf16[32,3,3584]{2,0,1:T(8,128)(2,1)S(1)} %copy.15) | copy-start | bytes 2064388
  80.1 10.5 %collective-permute-start = (bf16[32,3,3584]{2,0,1:T(8,128)(2,1)S(1)}, bf16[32,3,3584]{2,0,1:T(8,128)(2,1)S(1)}, u32[]{:S(2)}, u32[]{:S(2)}) collective-permute-start(bf16[32,3,3584]{2,0,1:T(8,128)(2,1)S(1)} %copy.15), channel_id=1, source_target_pairs={{0,32},{32,64},{64,96},{96,128},{128,160},{160,192},{192,224},{224... | collective-permute-start | bytes 2064392 | tf_op jit(solution)/shard_map/ppermute | solution.py:21
  90.5 11.6 %collective-permute-start.1 = (bf16[32,3,3584]{2,0,1:T(8,128)(2,1)S(1)}, bf16[32,3,3584]{2,0,1:T(8,128)(2,1)S(1)}, u32[]{:S(2)}, u32[]{:S(2)}) collective-permute-start(bf16[32,3,3584]{2,0,1:T(8,128)(2,1)S(1)} %collective-permute-done), channel_id=1, source_target_pairs={{0,32},{32,64},{64,96},{96,128},{128,160},{160,192},{192,224},{224... | collective-permute-start | bytes 2064392 | tf_op jit(solution)/shard_map/ppermute | solution.py:21
  95.2 176.1 %reduce-scatter.2.cloned.1.call-start = ((), (), s32[]{:S(2)}) async-start(), calls=%async_computation.4 | async-start | bytes 6193152 | tf_op jit(solution)/shard_map/reduce_scatter | solution.py:99
  95.3 14.6 %collective-permute-start.4 = (bf16[32,3,3584]{2,0,1:T(8,128)(2,1)}, bf16[32,3,3584]{2,0,1:T(8,128)(2,1)}, u32[]{:S(2)}, u32[]{:S(2)}) collective-permute-start(bf16[32,3,3584]{2,0,1:T(8,128)(2,1)} %copy-done.4), channel_id=1, source_target_pairs={{32,0},{64,32},{96,64},{128,96},{160,128},{192,160},{224,192},{0,2... | collective-permute-start | bytes 2064392 | tf_op jit(solution)/shard_map/ppermute | solution.py:23
  102.1 26.4 %collective-permute-start.2 = (bf16[32,3,3584]{2,0,1:T(8,128)(2,1)S(1)}, bf16[32,3,3584]{2,0,1:T(8,128)(2,1)}, u32[]{:S(2)}, u32[]{:S(2)}) collective-permute-start(bf16[32,3,3584]{2,0,1:T(8,128)(2,1)S(1)} %collective-permute-done.1), channel_id=1, source_target_pairs={{0,32},{32,64},{64,96},{96,128},{128,160},{160,192},{192,224},{224... | collective-permute-start | bytes 2064392 | tf_op jit(solution)/shard_map/ppermute | solution.py:21
  109.9 39.7 %collective-permute-start.5 = (bf16[32,3,3584]{2,0,1:T(8,128)(2,1)}, bf16[32,3,3584]{2,0,1:T(8,128)(2,1)}, u32[]{:S(2)}, u32[]{:S(2)}) collective-permute-start(bf16[32,3,3584]{2,0,1:T(8,128)(2,1)} %collective-permute-done.4), channel_id=1, source_target_pairs={{32,0},{64,32},{96,64},{128,96},{160,128},{192,160},{224,192},{0,2... | collective-permute-start | bytes 2064392 | tf_op jit(solution)/shard_map/ppermute | solution.py:23
  128.5 21.4 %collective-permute-start.3 = (bf16[32,3,3584]{2,0,1:T(8,128)(2,1)}, bf16[32,3,3584]{2,0,1:T(8,128)(2,1)}, u32[]{:S(2)}, u32[]{:S(2)}) collective-permute-start(bf16[32,3,3584]{2,0,1:T(8,128)(2,1)} %collective-permute-done.2), channel_id=1, source_target_pairs={{0,32},{32,64},{64,96},{96,128},{128,160},{160,192},{192,224},{224... | collective-permute-start | bytes 2064392 | tf_op jit(solution)/shard_map/ppermute | solution.py:21
  149.7 16.2 %collective-permute-start.6 = (bf16[32,3,3584]{2,0,1:T(8,128)(2,1)}, bf16[32,3,3584]{2,0,1:T(8,128)(2,1)S(1)}, u32[]{:S(2)}, u32[]{:S(2)}) collective-permute-start(bf16[32,3,3584]{2,0,1:T(8,128)(2,1)} %collective-permute-done.5), channel_id=1, source_target_pairs={{32,0},{64,32},{96,64},{128,96},{160,128},{192,160},{224,192},{0,2... | collective-permute-start | bytes 2064392 | tf_op jit(solution)/shard_map/ppermute | solution.py:23
  215.4 4.3 %copy-start.2 = (bf16[768,3584]{1,0:T(8,128)(2,1)S(1)}, bf16[768,3584]{1,0:T(8,128)(2,1)}, u32[]{:S(2)}) copy-start(bf16[768,3584]{1,0:T(8,128)(2,1)} %reshape.168) | copy-start | bytes 16515076
  215.4 7.8 %slice-start = ((s8[5505024]{0:T(1024)(128)(4,1)}), s8[4194304]{0:T(1024)(128)(4,1)S(1)}, s32[]{:S(2)}) async-start(s8[5505024]{0:T(1024)(128)(4,1)} %bitcast.61), calls=%async_computation.5 | async-start | bytes 8388608
  219.8 5.4 %copy-start.7 = (f32[768,256]{1,0:T(8,128)}, f32[768,256]{1,0:T(8,128)S(1)}, u32[]{:S(2)}) copy-start(f32[768,256]{1,0:T(8,128)S(1)} %fusion.5) | copy-start | bytes 2359300
  219.8 3.5 %slice-start.1 = ((s8[5505024]{0:T(1024)(128)(4,1)}), s8[1310720]{0:T(1024)(128)(4,1)S(1)}, s32[]{:S(2)}) async-start(s8[5505024]{0:T(1024)(128)(4,1)} %bitcast.61), calls=%async_computation.6 | async-start | bytes 2621440
  219.8 3.5 %copy-start.6 = (bf16[1,256,3584]{2,1,0:T(8,128)(2,1)S(1)}, bf16[1,256,3584]{2,1,0:T(8,128)(2,1)}, u32[]{:S(2)}) copy-start(bf16[1,256,3584]{2,1,0:T(8,128)(2,1)} %param.13) | copy-start | bytes 5505028
  223.3 1.8 copy-start.9
  225.1 1.7 copy-start.5
  225.2 1.7 copy-start.3
  271.3 17.5 %slice-start.4 = ((s8[5505024]{0:T(1024)(128)(4,1)}), s8[1310720]{0:T(1024)(128)(4,1)S(1)}, s32[]{:S(2)}) async-start(s8[5505024]{0:T(1024)(128)(4,1)} %bitcast.65), calls=%async_computation.9 | async-start | bytes 2621440
  273.5 34.3 %all-to-all-start.1 = ((bf16[32,3,3584]{2,1,0:T(4,128)(2,1)}), bf16[32,3,3584]{2,1,0:T(4,128)(2,1)}, u32[]{:S(2)}, u32[]{:S(2)}) async-start(bf16[32,3,3584]{2,1,0:T(4,128)(2,1)} %convert_element_type.49), calls=%async_computation.2 | async-start | bytes 1835008 | tf_op jit(solution)/shard_map/all_to_all | solution.py:108
  283.2 5.7 %slice-start.5 = ((s8[5505024]{0:T(1024)(128)(4,1)}), s8[4194304]{0:T(1024)(128)(4,1)S(1)}, s32[]{:S(2)}) async-start(s8[5505024]{0:T(1024)(128)(4,1)} %bitcast.65), calls=%async_computation.10 | async-start | bytes 8388608
  283.2 8.6 %slice-start.2 = ((s8[5505024]{0:T(1024)(128)(4,1)}), s8[4194304]{0:T(1024)(128)(4,1)S(1)}, s32[]{:S(2)}) async-start(s8[5505024]{0:T(1024)(128)(4,1)} %bitcast.63), calls=%async_computation.7 | async-start | bytes 8388608
  288.8 2.9 slice-start.3
  288.8 2.9 copy-start.8
  288.9 2.9 copy-start.10
Sparse Core Ops, SparseCore 0:
  95.3 44.0 all-gather.2
  231.0 40.2 reduce-scatter.1
